TPU v7x, 128 devices: a whole 4x4x4 slice. The times are simulated.
128 devices in a mesh: row: 16 (over y, z), col: 8 (over x, core).
Axes of the slice: x: 4, y: 4, z: 4, core: 2. Of those that a mesh axis runs over, the one named last changes fastest.
Arguments:
- right_side: bfloat16 [8, 16, 8, 128, 512], P(None, 'row', 'col'), may hold values from -6 to 6
- diag_inverse: bfloat16 [8, 16, 8, 128, 128], P(None, 'row', 'col'), may hold values from -1.5 to 1.5, as said below
- factor: bfloat16 [7, 16, 16, 8, 4, 128, 128], P(None, None, 'row', 'col'), may hold values from -0.0625 to 0.0625
- sources: int32 [7, 16, 16, 8, 4], P(None, None, 'row', 'col'), may hold values from 0 to 55, as said below
Outputs:
- solution: float32 [8, 16, 8, 128, 512], P(None, 'row', 'col')
Inputs may be any that keep to these rules, and one draw needn't show every extreme that they name: `diag_inverse`: each block is the inverse of a lower triangular diagonal block of the factor, hence lower triangular. `sources`: for a target of level l (first index l - 1), each entry numbers a solved block of a level below l in the same source grid row r as level * 8 + grid column. The 4 entries of one target, source grid row and target grid column are distinct; the first 2 lie in level l - 1 and the last 2 in levels below l - 1, except for l = 1, where all lie in level 0.
All inputs are finite; a program needn't handle non-finite values.
Results may differ from a plain program's by a relative error of at most 0.008.
Values may be sent and summed in bfloat16 or wider, within the bound.
No kernel may reach another device: no remote copies, remote signals or barrier semaphores. Data moves between devices by JAX's collectives and lax.ppermute only.
A program may use at most 192 MiB of HBM per device.

v0:
```python
import jax
import jax.numpy as jnp
from jax import lax
from jax.sharding import PartitionSpec as P


def broadcast_solved(solved_block):
    return lax.all_gather(solved_block[None], "col", axis=0, tiled=True)


def reduce_updates(update_term):
    return lax.psum_scatter(
        update_term(jnp.int32(0), 1 * lax.axis_size("row")), "row", scatter_dimension=0, tiled=True
    )


def contribute(blocks, source_pool, source_ids):
    picked = jnp.take(source_pool, source_ids, axis=0)
    return jnp.einsum("tkab,tkbn->tan", blocks, picked, preferred_element_type=jnp.float32)


def make_term(blocks, source_pool, source_ids):

    def update_term(first_row, row_count):
        return contribute(blocks, source_pool, source_ids)

    return update_term


def solve_columns(right_side, diag_inverse, factor, sources, col_first, col_last):
    level_total = right_side.shape[0]
    history = []
    solution_list = []
    for level_index in range(level_total):
        own_side = right_side[level_index, 0, 0, :, col_first:col_last]
        if level_index == 0:
            reduced = own_side
        else:
            blocks = factor[level_index - 1, :, 0, 0]
            source_ids = sources[level_index - 1, :, 0, 0, :]
            source_pool = jnp.concatenate(history, axis=0)
            update = reduce_updates(make_term(blocks, source_pool, source_ids))
            reduced = (own_side.astype(jnp.float32) - update[0]).astype(jnp.bfloat16)
        solution = jnp.dot(
            diag_inverse[level_index, 0, 0], reduced, preferred_element_type=jnp.float32
        )
        solution_list.append(solution)
        if level_index + 1 < level_total:
            history.append(broadcast_solved(solution.astype(jnp.bfloat16)))
    return jnp.stack(solution_list)


def per_device(right_side, diag_inverse, factor, sources):
    col_total = right_side.shape[-1]
    solution = solve_columns(right_side, diag_inverse, factor, sources, 0, col_total)
    return solution[:, None, None]


def solution(mesh):
    placed = (
        P(None, "row", "col", None, None),
        P(None, "row", "col", None, None),
        P(None, None, "row", "col", None, None, None),
        P(None, None, "row", "col", None),
    )
    return jax.shard_map(
        per_device,
        mesh=mesh,
        in_specs=placed,
        out_specs=P(None, "row", "col", None, None),
        check_vma=False,
    )
```

profile of v0, /device:TPU:0, one launch (start us, length us, event | category | flops | bytes accessed | tf_op | source)
XLA Modules:
  0.0 952.0 jit_solution(17876641875087454846)
XLA Ops:
  11.5 23.3 %all-gather.15.cloned.1.call-done = bf16[1024,512]{1,0:T(8,128)(2,1)} async-done(((bf16[128,512]{1,0:T(8,128)(2,1)}), bf16[1024,512]{1,0:T(8,128)(2,1)}) %all-gather.15.cloned.1.call-update) | async-done | bytes 1048592 | tf_op jit(solution)/shard_map/all_gather | solution.py:8
  41.5 12.0 %copy.94 = bf16[64,128,512]{1,2,0:T(8,128)(2,1)} copy(bf16[64,128,512]{2,1,0:T(8,128)(2,1)} %gather_fusion) | data formatting | bytes 16777216 | tf_op jit(solution)/shard_map/jit(_take)/gather | solution.py:18
  53.5 8.5 fusion.28
  63.0 77.8 %reduce-scatter.22.cloned.1.call-done = f32[1,128,512]{1,2,0:T(8,128)} async-done(((f32[16,128,512]{1,2,0:T(8,128)}), f32[1,128,512]{1,2,0:T(8,128)}) %reduce-scatter.22.cloned.1.call-update) | async-done | bytes 262160
  143.6 21.5 %all-gather.17.cloned.1.call-done = bf16[1024,512]{1,0:T(8,128)(2,1)} async-done(((bf16[128,512]{1,0:T(8,128)(2,1)}), bf16[1024,512]{1,0:T(8,128)(2,1)}) %all-gather.17.cloned.1.call-update) | async-done | bytes 1048592 | tf_op jit(solution)/shard_map/all_gather | solution.py:8
  172.1 12.0 %copy.100 = bf16[64,128,512]{1,2,0:T(8,128)(2,1)} copy(bf16[64,128,512]{2,1,0:T(8,128)(2,1)} %gather_fusion.1) | data formatting | bytes 16777216 | tf_op jit(solution)/shard_map/jit(_take)/gather | solution.py:18
  184.1 8.5 fusion.31
  192.8 78.5 %reduce-scatter.24.cloned.1.call-done = f32[1,128,512]{1,2,0:T(8,128)} async-done(((f32[16,128,512]{1,2,0:T(8,128)}), f32[1,128,512]{1,2,0:T(8,128)}) %reduce-scatter.24.cloned.1.call-update) | async-done | bytes 262160
  274.1 21.5 %all-gather.19.cloned.1.call-done = bf16[1024,512]{1,0:T(8,128)(2,1)} async-done(((bf16[128,512]{1,0:T(8,128)(2,1)}), bf16[1024,512]{1,0:T(8,128)(2,1)}) %all-gather.19.cloned.1.call-update) | async-done | bytes 1048592 | tf_op jit(solution)/shard_map/all_gather | solution.py:8
  305.9 12.0 %copy.106 = bf16[64,128,512]{1,2,0:T(8,128)(2,1)} copy(bf16[64,128,512]{2,1,0:T(8,128)(2,1)} %gather_fusion.2) | data formatting | bytes 16777216 | tf_op jit(solution)/shard_map/jit(_take)/gather | solution.py:18
  328.2 77.0 %reduce-scatter.26.cloned.1.call-done = f32[1,128,512]{1,2,0:T(8,128)} async-done(((f32[16,128,512]{1,2,0:T(8,128)}), f32[1,128,512]{1,2,0:T(8,128)}) %reduce-scatter.26.cloned.1.call-update) | async-done | bytes 262160
  410.1 19.5 %all-gather.21.cloned.1.call-done = bf16[1024,512]{1,0:T(8,128)(2,1)} async-done(((bf16[128,512]{1,0:T(8,128)(2,1)}), bf16[1024,512]{1,0:T(8,128)(2,1)}) %all-gather.21.cloned.1.call-update) | async-done | bytes 1048592 | tf_op jit(solution)/shard_map/all_gather | solution.py:8
  440.8 11.9 %copy.112 = bf16[64,128,512]{1,2,0:T(8,128)(2,1)} copy(bf16[64,128,512]{2,1,0:T(8,128)(2,1)} %gather_fusion.3) | data formatting | bytes 16777216 | tf_op jit(solution)/shard_map/jit(_take)/gather | solution.py:18
  462.7 77.0 %reduce-scatter.28.cloned.1.call-done = f32[1,128,512]{1,2,0:T(8,128)} async-done(((f32[16,128,512]{1,2,0:T(8,128)}), f32[1,128,512]{1,2,0:T(8,128)}) %reduce-scatter.28.cloned.1.call-update) | async-done | bytes 262160
  553.8 10.4 %all-gather.23.cloned.1.call-done = bf16[1024,512]{1,0:T(8,128)(2,1)} async-done(((bf16[128,512]{1,0:T(8,128)(2,1)}), bf16[1024,512]{1,0:T(8,128)(2,1)}) %all-gather.23.cloned.1.call-update) | async-done | bytes 1048592 | tf_op jit(solution)/shard_map/all_gather | solution.py:8
  575.6 12.0 %copy.118 = bf16[64,128,512]{1,2,0:T(8,128)(2,1)} copy(bf16[64,128,512]{2,1,0:T(8,128)(2,1)} %gather_fusion.4) | data formatting | bytes 16777216 | tf_op jit(solution)/shard_map/jit(_take)/gather | solution.py:18
  596.2 78.6 %reduce-scatter.30.cloned.1.call-done = f32[1,128,512]{1,2,0:T(8,128)} async-done(((f32[16,128,512]{1,2,0:T(8,128)}), f32[1,128,512]{1,2,0:T(8,128)}) %reduce-scatter.30.cloned.1.call-update) | async-done | bytes 262160
  677.1 22.0 %all-gather.25.cloned.1.call-done = bf16[1024,512]{1,0:T(8,128)(2,1)} async-done(((bf16[128,512]{1,0:T(8,128)(2,1)}), bf16[1024,512]{1,0:T(8,128)(2,1)}) %all-gather.25.cloned.1.call-update) | async-done | bytes 1048592 | tf_op jit(solution)/shard_map/all_gather | solution.py:8
  710.2 11.9 %copy.124 = bf16[64,128,512]{1,2,0:T(8,128)(2,1)} copy(bf16[64,128,512]{2,1,0:T(8,128)(2,1)} %gather_fusion.5) | data formatting | bytes 16777216 | tf_op jit(solution)/shard_map/jit(_take)/gather | solution.py:18
  730.6 78.6 %reduce-scatter.32.cloned.1.call-done = f32[1,128,512]{1,2,0:T(8,128)} async-done(((f32[16,128,512]{1,2,0:T(8,128)}), f32[1,128,512]{1,2,0:T(8,128)}) %reduce-scatter.32.cloned.1.call-update) | async-done | bytes 262160
  811.5 22.1 %all-gather.27.cloned.1.call-done = bf16[1024,512]{1,0:T(8,128)(2,1)} async-done(((bf16[128,512]{1,0:T(8,128)(2,1)}), bf16[1024,512]{1,0:T(8,128)(2,1)}) %all-gather.27.cloned.1.call-update) | async-done | bytes 1048592 | tf_op jit(solution)/shard_map/all_gather | solution.py:8
  835.9 8.7 gather_fusion.6
  844.5 11.9 %copy.130 = bf16[64,128,512]{1,2,0:T(8,128)(2,1)} copy(bf16[64,128,512]{2,1,0:T(8,128)(2,1)} %gather_fusion.6) | data formatting | bytes 16777216 | tf_op jit(solution)/shard_map/jit(_take)/gather | solution.py:18
  864.9 78.6 %reduce-scatter.34.cloned.1.call-done = f32[1,128,512]{1,2,0:T(8,128)} async-done(((f32[16,128,512]{1,2,0:T(8,128)}), f32[1,128,512]{1,2,0:T(8,128)}) %reduce-scatter.34.cloned.1.call-update) | async-done | bytes 262160
  (118 shorter events, 142.7 us)
Async XLA Ops:
  6.5 28.2 %all-gather.15.cloned.1.call-start = ((), (), s32[]{:S(2)}) async-start(), calls=%async_computation.7 | async-start | bytes 1179648 | tf_op jit(solution)/shard_map/all_gather | solution.py:8
  8.4 132.4 %reduce-scatter.22.cloned.1.call-start = ((), (), s32[]{:S(2)}) async-start(), calls=%async_computation.14 | async-start | bytes 4456448
  62.0 103.1 %copy-start = (bf16[1024,512]{1,0:T(8,128)(2,1)S(1)}, bf16[1024,512]{1,0:T(8,128)(2,1)}, u32[]{:S(2)}) copy-start(bf16[1024,512]{1,0:T(8,128)(2,1)} %all-gather.15.cloned.1.call-done) | copy-start | bytes 3145732
  62.1 103.1 %all-gather.17.cloned.1.call-start = ((), (), s32[]{:S(2)}) async-start(), calls=%async_computation.8 | async-start | bytes 1179648 | tf_op jit(solution)/shard_map/all_gather | solution.py:8
  142.7 128.6 %reduce-scatter.24.cloned.1.call-start = ((), (), s32[]{:S(2)}) async-start(), calls=%async_computation.15 | async-start | bytes 4456448
  172.1 12.0 %copy-start.10 = (pred[16,4]{1,0:T(8,128)(4,1)S(1)}, pred[16,4]{1,0:T(8,128)(4,1)}, u32[]{:S(2)}) copy-start(pred[16,4]{1,0:T(8,128)(4,1)} %copy.98) | copy-start | bytes 196
  184.1 8.6 copy-start.5
  184.1 89.3 %copy-start.8 = (pred[16,4]{0,1:T(4,128)(4,1)S(1)}, pred[16,4]{0,1:T(4,128)(4,1)}, u32[]{:S(2)}) copy-start(pred[16,4]{0,1:T(4,128)(4,1)} %get-tuple-element.32) | copy-start | bytes 196
  184.1 111.6 %copy-start.1 = (bf16[1024,512]{1,0:T(8,128)(2,1)S(1)}, bf16[1024,512]{1,0:T(8,128)(2,1)}, u32[]{:S(2)}) copy-start(bf16[1024,512]{1,0:T(8,128)(2,1)} %all-gather.17.cloned.1.call-done) | copy-start | bytes 3145732
  192.6 103.0 %all-gather.19.cloned.1.call-start = ((), (), s32[]{:S(2)}) async-start(), calls=%async_computation.9 | async-start | bytes 1179648 | tf_op jit(solution)/shard_map/all_gather | solution.py:8
  273.2 132.0 %reduce-scatter.26.cloned.1.call-start = ((), (), s32[]{:S(2)}) async-start(), calls=%async_computation.16 | async-start | bytes 4456448
  305.9 12.0 %copy-start.11 = (pred[16,4]{1,0:T(8,128)(4,1)S(1)}, pred[16,4]{1,0:T(8,128)(4,1)}, u32[]{:S(2)}) copy-start(pred[16,4]{1,0:T(8,128)(4,1)} %copy.104) | copy-start | bytes 196
  317.9 111.7 %copy-start.2 = (bf16[1024,512]{1,0:T(8,128)(2,1)S(1)}, bf16[1024,512]{1,0:T(8,128)(2,1)}, u32[]{:S(2)}) copy-start(bf16[1024,512]{1,0:T(8,128)(2,1)} %all-gather.19.cloned.1.call-done) | copy-start | bytes 3145732
  326.5 103.1 %all-gather.21.cloned.1.call-start = ((), (), s32[]{:S(2)}) async-start(), calls=%async_computation.10 | async-start | bytes 1179648 | tf_op jit(solution)/shard_map/all_gather | solution.py:8
  407.2 132.6 %reduce-scatter.28.cloned.1.call-start = ((), (), s32[]{:S(2)}) async-start(), calls=%async_computation.17 | async-start | bytes 4456448
  461.0 103.1 %all-gather.23.cloned.1.call-start = ((), (), s32[]{:S(2)}) async-start(), calls=%async_computation.11 | async-start | bytes 1179648 | tf_op jit(solution)/shard_map/all_gather | solution.py:8
  541.7 133.1 %reduce-scatter.30.cloned.1.call-start = ((), (), s32[]{:S(2)}) async-start(), calls=%async_computation.18 | async-start | bytes 4456448
  575.6 12.0 %copy-start.9 = (pred[16,4]{1,0:T(8,128)(4,1)S(1)}, pred[16,4]{1,0:T(8,128)(4,1)}, u32[]{:S(2)}) copy-start(pred[16,4]{1,0:T(8,128)(4,1)} %copy.116) | copy-start | bytes 196
  587.6 89.4 %copy-start.7 = (pred[16,4]{0,1:T(4,128)(4,1)S(1)}, pred[16,4]{0,1:T(4,128)(4,1)}, u32[]{:S(2)}) copy-start(pred[16,4]{0,1:T(4,128)(4,1)} %get-tuple-element.35) | copy-start | bytes 196
  596.0 103.1 %all-gather.25.cloned.1.call-start = ((), (), s32[]{:S(2)}) async-start(), calls=%async_computation.12 | async-start | bytes 1179648 | tf_op jit(solution)/shard_map/all_gather | solution.py:8
  676.7 132.6 %reduce-scatter.32.cloned.1.call-start = ((), (), s32[]{:S(2)}) async-start(), calls=%async_computation.19 | async-start | bytes 4456448
  722.1 89.3 %copy-start.6 = (pred[16,4]{0,1:T(4,128)(4,1)S(1)}, pred[16,4]{0,1:T(4,128)(4,1)}, u32[]{:S(2)}) copy-start(pred[16,4]{0,1:T(4,128)(4,1)} %get-tuple-element.29) | copy-start | bytes 196
  730.5 103.1 %all-gather.27.cloned.1.call-start = ((), (), s32[]{:S(2)}) async-start(), calls=%async_computation.13 | async-start | bytes 1179648 | tf_op jit(solution)/shard_map/all_gather | solution.py:8
  811.2 132.4 %reduce-scatter.34.cloned.1.call-start = ((), (), s32[]{:S(2)}) async-start(), calls=%async_computation.20 | async-start | bytes 4456448
  (2 other events, 15.0 us)
Sparse Core Ops, SparseCore 0:
  9.0 25.6 all-gather.14
  62.2 78.5 reduce-scatter.21
  142.8 22.2 all-gather.16
  192.8 78.4 reduce-scatter.23
  273.3 22.2 all-gather.18
  326.6 78.5 reduce-scatter.25
  407.3 22.2 all-gather.20
  461.1 78.5 reduce-scatter.27
  541.8 22.2 all-gather.22
  596.1 78.6 reduce-scatter.29
  676.8 22.2 all-gather.24
  730.6 78.6 reduce-scatter.31
  811.3 22.2 all-gather.26
  864.9 78.6 reduce-scatter.33
where the time goes:
time: 955 us; the launch traced here: 952 us
  waiting for transfers between devices  687 us (72%)
  local copies, waits for them, and re-layouts  165 us (17%)
  matrix products  74.1 us (8%)
  between operations  13.4 us (1%)
  other arithmetic  11.7 us (1%)
    unnamed x21, waiting for transfers between devices  546 us
    all_gather x7, waiting for transfers between devices, broadcast_solved(): return lax.all_gather(solved_block[None], 'col', axis=0, tiled=True)  140 us
    gather x14, local copies, waits for them, and re-layouts, contribute(): picked = jnp.take(source_pool, source_ids, axis=0)  136 us
    dot_general x7, matrix products, contribute(): jnp.einsum('tkab,tkbn->tan', blocks, picked, preferred_element_type=jnp.f...  58.9 us
  transfers between devices with their start and end apart: 14, of which 14 were waited for; matrix products, arithmetic and copies ran while one was open for 3% of the time, Pallas kernels for 0%

commit v1 on v0

--- a/solution.py
+++ b/solution.py
@@ -5,7 +5,9 @@
 
 
 def broadcast_solved(solved_block):
-    return lax.all_gather(solved_block[None], "col", axis=0, tiled=True)
+    return jnp.concatenate(
+        lax.all_to_all(jnp.stack([solved_block[None]] * lax.axis_size("col")), "col", 0, 0), axis=0
+    )
 
 
 def reduce_updates(update_term):

time: 955 us -> 924 us (0.968)
  waiting for transfers between devices: 687 us -> 620 us
  starting transfers between devices: 0.95 us -> 30.8 us
    all_gather x7 -> x0, waiting for transfers between devices: 140 us -> none  [broadcast_solved(): return lax.all_gather(solved_block[None], 'col', axis=0, tiled=True)]
    all_to_all x0 -> x7, waiting for transfers between devices: none -> 93.2 us  [broadcast_solved(): lax.all_to_all(jnp.stack([solved_block[None]] * lax.axis_size('col')), 'c...]
    all_to_all x0 -> x7, starting transfers between devices: none -> 29.9 us  [broadcast_solved(): lax.all_to_all(jnp.stack([solved_block[None]] * lax.axis_size('col')), 'c...]
    unnamed x21 -> x14, waiting for transfers between devices: 546 us -> 527 us
where the time goes in v1:
time: 924 us; the launch traced here: 921 us
  waiting for transfers between devices  620 us (67%)
  local copies, waits for them, and re-layouts  172 us (19%)
  matrix products  73.4 us (8%)
  starting transfers between devices  30.8 us (3%)
  between operations  13.6 us (1%)
  other arithmetic  11.3 us (1%)
    unnamed x14, waiting for transfers between devices  527 us
    gather x14, local copies, waits for them, and re-layouts, contribute(): picked = jnp.take(source_pool, source_ids, axis=0)  137 us
    all_to_all x7, waiting for transfers between devices, broadcast_solved(): lax.all_to_all(jnp.stack([solved_block[None]] * lax.axis_size('col')), 'c...  93.2 us
    dot_general x7, matrix products, contribute(): jnp.einsum('tkab,tkbn->tan', blocks, picked, preferred_element_type=jnp.f...  58.5 us
    all_to_all x7, starting transfers between devices, broadcast_solved(): lax.all_to_all(jnp.stack([solved_block[None]] * lax.axis_size('col')), 'c...  29.9 us
  transfers between devices with their start and end apart: 14, of which 14 were waited for; matrix products, arithmetic and copies ran while one was open for 3% of the time, Pallas kernels for 0%

profile of v1, /device:TPU:0, one launch (start us, length us, event | category | flops | bytes accessed | tf_op | source)
XLA Modules:
  0.0 921.2 jit_solution(5509230085931677026)
XLA Ops:
  16.9 12.8 %all-to-all-done = bf16[8,1,128,512]{3,2,1,0:T(8,128)(2,1)S(1)} async-done(((bf16[8,1,128,512]{3,2,1,0:T(8,128)(2,1)}), bf16[8,1,128,512]{3,2,1,0:T(8,128)(2,1)S(1)}, u32[]{:S(2)}, u32[]{:S(2)}) %all-to-all-start) | async-done | bytes 1048608 | tf_op jit(solution)/shard_map/all_to_all | solution.py:9
  35.3 12.2 %copy.87 = bf16[16,4,128,512]{2,3,1,0:T(8,128)(2,1)} copy(bf16[16,4,128,512]{3,2,1,0:T(8,128)(2,1)} %bitcast.339) | data formatting | bytes 16777216 | tf_op jit(solution)/shard_map/jit(_take)/gather | solution.py:20
  47.5 8.4 fusion.28
  56.9 78.4 %reduce-scatter.22.cloned.1.call-done = f32[1,128,512]{1,2,0:T(8,128)} async-done(((f32[16,128,512]{1,2,0:T(8,128)}), f32[1,128,512]{1,2,0:T(8,128)}) %reduce-scatter.22.cloned.1.call-update) | async-done | bytes 262160
  143.4 15.0 %all-to-all-done.1 = bf16[8,1,128,512]{3,2,1,0:T(8,128)(2,1)S(1)} async-done(((bf16[8,1,128,512]{3,2,1,0:T(8,128)(2,1)}), bf16[8,1,128,512]{3,2,1,0:T(8,128)(2,1)S(1)}, u32[]{:S(2)}, u32[]{:S(2)}) %all-to-all-start.1) | async-done | bytes 1048608 | tf_op jit(solution)/shard_map/all_to_all | solution.py:9
  166.4 12.2 %copy.93 = bf16[16,4,128,512]{2,3,1,0:T(8,128)(2,1)} copy(bf16[16,4,128,512]{3,2,1,0:T(8,128)(2,1)} %bitcast.333) | data formatting | bytes 16777216 | tf_op jit(solution)/shard_map/jit(_take)/gather | solution.py:20
  178.6 8.4 fusion.31
  187.2 76.0 %reduce-scatter.24.cloned.1.call-done = f32[1,128,512]{1,2,0:T(8,128)} async-done(((f32[16,128,512]{1,2,0:T(8,128)}), f32[1,128,512]{1,2,0:T(8,128)}) %reduce-scatter.24.cloned.1.call-update) | async-done | bytes 262160
  273.3 13.0 %all-to-all-done.2 = bf16[8,1,128,512]{3,2,1,0:T(8,128)(2,1)S(1)} async-done(((bf16[8,1,128,512]{3,2,1,0:T(8,128)(2,1)}), bf16[8,1,128,512]{3,2,1,0:T(8,128)(2,1)S(1)}, u32[]{:S(2)}, u32[]{:S(2)}) %all-to-all-start.2) | async-done | bytes 1048608 | tf_op jit(solution)/shard_map/all_to_all | solution.py:9
  295.6 12.2 %copy.99 = bf16[16,4,128,512]{2,3,1,0:T(8,128)(2,1)} copy(bf16[16,4,128,512]{3,2,1,0:T(8,128)(2,1)} %bitcast.334) | data formatting | bytes 16777216 | tf_op jit(solution)/shard_map/jit(_take)/gather | solution.py:20
  317.8 74.5 %reduce-scatter.26.cloned.1.call-done = f32[1,128,512]{1,2,0:T(8,128)} async-done(((f32[16,128,512]{1,2,0:T(8,128)}), f32[1,128,512]{1,2,0:T(8,128)}) %reduce-scatter.26.cloned.1.call-update) | async-done | bytes 262160
  402.4 13.1 %all-to-all-done.3 = bf16[8,1,128,512]{3,2,1,0:T(8,128)(2,1)} async-done(((bf16[8,1,128,512]{3,2,1,0:T(8,128)(2,1)}), bf16[8,1,128,512]{3,2,1,0:T(8,128)(2,1)}, u32[]{:S(2)}, u32[]{:S(2)}) %all-to-all-start.3) | async-done | bytes 1048608 | tf_op jit(solution)/shard_map/all_to_all | solution.py:9
  426.7 12.2 %copy.105 = bf16[16,4,128,512]{2,3,1,0:T(8,128)(2,1)} copy(bf16[16,4,128,512]{3,2,1,0:T(8,128)(2,1)} %bitcast.335) | data formatting | bytes 16777216 | tf_op jit(solution)/shard_map/jit(_take)/gather | solution.py:20
  453.6 69.7 %reduce-scatter.28.cloned.1.call-done = f32[1,128,512]{1,2,0:T(8,128)} async-done(((f32[16,128,512]{1,2,0:T(8,128)}), f32[1,128,512]{1,2,0:T(8,128)}) %reduce-scatter.28.cloned.1.call-update) | async-done | bytes 262160
  538.2 8.3 all-to-all-done.4
  556.6 12.2 %copy.111 = bf16[16,4,128,512]{2,3,1,0:T(8,128)(2,1)} copy(bf16[16,4,128,512]{3,2,1,0:T(8,128)(2,1)} %bitcast.336) | data formatting | bytes 16777216 | tf_op jit(solution)/shard_map/jit(_take)/gather | solution.py:20
  577.3 76.1 %reduce-scatter.30.cloned.1.call-done = f32[1,128,512]{1,2,0:T(8,128)} async-done(((f32[16,128,512]{1,2,0:T(8,128)}), f32[1,128,512]{1,2,0:T(8,128)}) %reduce-scatter.30.cloned.1.call-update) | async-done | bytes 262160
  660.9 15.6 %all-to-all-done.5 = bf16[8,1,128,512]{3,2,1,0:T(8,128)(2,1)S(1)} async-done(((bf16[8,1,128,512]{3,2,1,0:T(8,128)(2,1)}), bf16[8,1,128,512]{3,2,1,0:T(8,128)(2,1)S(1)}, u32[]{:S(2)}, u32[]{:S(2)}) %all-to-all-start.5) | async-done | bytes 1048608 | tf_op jit(solution)/shard_map/all_to_all | solution.py:9
  686.4 12.2 %copy.117 = bf16[16,4,128,512]{2,3,1,0:T(8,128)(2,1)} copy(bf16[16,4,128,512]{3,2,1,0:T(8,128)(2,1)} %bitcast.337) | data formatting | bytes 16777216 | tf_op jit(solution)/shard_map/jit(_take)/gather | solution.py:20
  707.1 76.0 %reduce-scatter.32.cloned.1.call-done = f32[1,128,512]{1,2,0:T(8,128)} async-done(((f32[16,128,512]{1,2,0:T(8,128)}), f32[1,128,512]{1,2,0:T(8,128)}) %reduce-scatter.32.cloned.1.call-update) | async-done | bytes 262160
  790.9 15.3 %all-to-all-done.6 = bf16[8,1,128,512]{3,2,1,0:T(8,128)(2,1)S(1)} async-done(((bf16[8,1,128,512]{3,2,1,0:T(8,128)(2,1)}), bf16[8,1,128,512]{3,2,1,0:T(8,128)(2,1)S(1)}, u32[]{:S(2)}, u32[]{:S(2)}) %all-to-all-start.6) | async-done | bytes 1048608 | tf_op jit(solution)/shard_map/all_to_all | solution.py:9
  807.2 8.6 gather_fusion.6
  815.9 12.2 %copy.123 = bf16[16,4,128,512]{2,3,1,0:T(8,128)(2,1)} copy(bf16[16,4,128,512]{3,2,1,0:T(8,128)(2,1)} %bitcast.338) | data formatting | bytes 16777216 | tf_op jit(solution)/shard_map/jit(_take)/gather | solution.py:20
  836.6 75.9 %reduce-scatter.34.cloned.1.call-done = f32[1,128,512]{1,2,0:T(8,128)} async-done(((f32[16,128,512]{1,2,0:T(8,128)}), f32[1,128,512]{1,2,0:T(8,128)}) %reduce-scatter.34.cloned.1.call-update) | async-done | bytes 262160
  (109 shorter events, 176.5 us)
Async XLA Ops:
  9.4 20.3 %all-to-all-start = ((bf16[8,1,128,512]{3,2,1,0:T(8,128)(2,1)}), bf16[8,1,128,512]{3,2,1,0:T(8,128)(2,1)S(1)}, u32[]{:S(2)}, u32[]{:S(2)}) async-start(bf16[8,1,128,512]{3,2,1,0:T(8,128)(2,1)} %stack.49), calls=%async_computation | async-start | bytes 2097152 | tf_op jit(solution)/shard_map/all_to_all | solution.py:9
  13.8 121.5 %reduce-scatter.22.cloned.1.call-start = ((), (), s32[]{:S(2)}) async-start(), calls=%async_computation.14 | async-start | bytes 4456448
  47.5 8.5 copy-start.2
  138.3 20.2 %all-to-all-start.1 = ((bf16[8,1,128,512]{3,2,1,0:T(8,128)(2,1)}), bf16[8,1,128,512]{3,2,1,0:T(8,128)(2,1)S(1)}, u32[]{:S(2)}, u32[]{:S(2)}) async-start(bf16[8,1,128,512]{3,2,1,0:T(8,128)(2,1)} %stack.51), calls=%async_computation.1 | async-start | bytes 2097152 | tf_op jit(solution)/shard_map/all_to_all | solution.py:9
  142.5 120.6 %reduce-scatter.24.cloned.1.call-start = ((), (), s32[]{:S(2)}) async-start(), calls=%async_computation.15 | async-start | bytes 4456448
  158.4 1.0 copy-start
  166.4 12.3 %copy-start.6 = (pred[16,4]{1,0:T(8,128)(4,1)S(1)}, pred[16,4]{1,0:T(8,128)(4,1)}, u32[]{:S(2)}) copy-start(pred[16,4]{1,0:T(8,128)(4,1)} %copy.91) | copy-start | bytes 196
  178.6 8.4 copy-start.3
  187.0 99.3 %copy-start.1 = (bf16[8,1,128,512]{3,2,1,0:T(8,128)(2,1)S(1)}, bf16[8,1,128,512]{3,2,1,0:T(8,128)(2,1)}, u32[]{:S(2)}) copy-start(bf16[8,1,128,512]{3,2,1,0:T(8,128)(2,1)} %copy-done) | copy-start | bytes 3145732
  266.1 20.2 %all-to-all-start.2 = ((bf16[8,1,128,512]{3,2,1,0:T(8,128)(2,1)}), bf16[8,1,128,512]{3,2,1,0:T(8,128)(2,1)S(1)}, u32[]{:S(2)}, u32[]{:S(2)}) async-start(bf16[8,1,128,512]{3,2,1,0:T(8,128)(2,1)} %stack.53), calls=%async_computation.2 | async-start | bytes 2097152 | tf_op jit(solution)/shard_map/all_to_all | solution.py:9
  270.3 122.0 %reduce-scatter.26.cloned.1.call-start = ((), (), s32[]{:S(2)}) async-start(), calls=%async_computation.16 | async-start | bytes 4456448
  395.3 20.3 %all-to-all-start.3 = ((bf16[8,1,128,512]{3,2,1,0:T(8,128)(2,1)}), bf16[8,1,128,512]{3,2,1,0:T(8,128)(2,1)}, u32[]{:S(2)}, u32[]{:S(2)}) async-start(bf16[8,1,128,512]{3,2,1,0:T(8,128)(2,1)} %stack.55), calls=%async_computation.3 | async-start | bytes 2097152 | tf_op jit(solution)/shard_map/all_to_all | solution.py:9
  399.6 123.8 %reduce-scatter.28.cloned.1.call-start = ((), (), s32[]{:S(2)}) async-start(), calls=%async_computation.17 | async-start | bytes 4456448
  526.4 20.2 %all-to-all-start.4 = ((bf16[8,1,128,512]{3,2,1,0:T(8,128)(2,1)}), bf16[8,1,128,512]{3,2,1,0:T(8,128)(2,1)S(1)}, u32[]{:S(2)}, u32[]{:S(2)}) async-start(bf16[8,1,128,512]{3,2,1,0:T(8,128)(2,1)} %stack.57), calls=%async_computation.4 | async-start | bytes 2097152 | tf_op jit(solution)/shard_map/all_to_all | solution.py:9
  530.6 122.8 %reduce-scatter.30.cloned.1.call-start = ((), (), s32[]{:S(2)}) async-start(), calls=%async_computation.18 | async-start | bytes 4456448
  577.2 83.6 %copy-start.5 = (pred[16,4]{0,1:T(4,128)(4,1)S(1)}, pred[16,4]{0,1:T(4,128)(4,1)}, u32[]{:S(2)}) copy-start(pred[16,4]{0,1:T(4,128)(4,1)} %get-tuple-element.35) | copy-start | bytes 196
  656.3 20.2 %all-to-all-start.5 = ((bf16[8,1,128,512]{3,2,1,0:T(8,128)(2,1)}), bf16[8,1,128,512]{3,2,1,0:T(8,128)(2,1)S(1)}, u32[]{:S(2)}, u32[]{:S(2)}) async-start(bf16[8,1,128,512]{3,2,1,0:T(8,128)(2,1)} %stack.59), calls=%async_computation.5 | async-start | bytes 2097152 | tf_op jit(solution)/shard_map/all_to_all | solution.py:9
  660.6 122.6 %reduce-scatter.32.cloned.1.call-start = ((), (), s32[]{:S(2)}) async-start(), calls=%async_computation.19 | async-start | bytes 4456448
  706.9 83.8 %copy-start.4 = (pred[16,4]{0,1:T(4,128)(4,1)S(1)}, pred[16,4]{0,1:T(4,128)(4,1)}, u32[]{:S(2)}) copy-start(pred[16,4]{0,1:T(4,128)(4,1)} %get-tuple-element.29) | copy-start | bytes 196
  786.0 20.2 %all-to-all-start.6 = ((bf16[8,1,128,512]{3,2,1,0:T(8,128)(2,1)}), bf16[8,1,128,512]{3,2,1,0:T(8,128)(2,1)S(1)}, u32[]{:S(2)}, u32[]{:S(2)}) async-start(bf16[8,1,128,512]{3,2,1,0:T(8,128)(2,1)} %stack.61), calls=%async_computation.6 | async-start | bytes 2097152 | tf_op jit(solution)/shard_map/all_to_all | solution.py:9
  790.3 122.3 %reduce-scatter.34.cloned.1.call-start = ((), (), s32[]{:S(2)}) async-start(), calls=%async_computation.20 | async-start | bytes 4456448
Sparse Core Ops, SparseCore 0:
  56.1 79.1 reduce-scatter.21
  187.2 75.9 reduce-scatter.23
  316.3 75.9 reduce-scatter.25
  447.4 75.9 reduce-scatter.27
  577.3 76.0 reduce-scatter.29
  707.1 75.9 reduce-scatter.31
  836.6 75.8 reduce-scatter.33
